TPU v7x, 256 devices: a whole 4x4x8 slice. The times are simulated.
256 devices in a mesh: ctx: 64 (over x_hi, y, z), tp: 4 (over x_lo, core).
Axes of the slice: x: 4 (x_hi: 2, x_lo: 2; x = x_hi * 2 + x_lo), y: 4, z: 8, core: 2. Of those that a mesh axis runs over, the one named last changes fastest.
Arguments:
- hidden: bfloat16 [32768, 5120], P('ctx', 'tp'), may hold values from -6 to 6
- queries: bfloat16 [32768, 5120], P('ctx', 'tp'), may hold values from -600 to 600
- lengths: int32 [256], replicated, may hold values from 1 to 2048, 32768 in all
- norm_gain: float32 [5120], P('tp'), may hold values from 0.5 to 1.5
- kv_weight: bfloat16 [5120, 2, 1024], P(None, None, 'tp'), may hold values from -0.078125 to 0.078125
- kv_bias: float32 [2, 1024], P(None, 'tp'), may hold values from -3 to 3
Outputs:
- attended: bfloat16 [32768, 5120], P('ctx', 'tp')
Inputs may be any that keep to these rules, and one draw needn't show every extreme that they name: The 256 files fill the 32768 positions in order; their lengths sum to 32768 and the longest is exactly 2048.
All inputs are finite; a program needn't handle non-finite values.
Results may differ from a plain program's by a relative error of at most 0.006.
Values may be sent and summed in bfloat16 or wider, within the bound.
A program may use at most 128 MiB of HBM per device.

v0:
```python
import jax
import jax.numpy as jnp
from jax import lax
from jax.sharding import PartitionSpec as P

D = 5120
HD = 128
CYCLE = 4


def shifted(value, axis, steps):
    count = lax.axis_size(axis)
    leading, last = (max(0, -steps), min(count, count - steps))
    return lax.ppermute(value, axis, [(source, source + steps) for source in range(leading, last)])


def body(hidden, queries, lengths, norm_gain, kv_weight, kv_bias):
    tok = hidden.shape[0]
    xfull = hidden.astype(jnp.float32)
    squares = lax.psum(jnp.sum(xfull * xfull, axis=1), "tp")
    scale_rows = lax.rsqrt(squares / D + 1e-06)
    normed = (xfull * scale_rows[:, None] * norm_gain[None, :]).astype(jnp.bfloat16)
    flat_weight = kv_weight.reshape(kv_weight.shape[0], -1)
    summed = jnp.dot(
        lax.all_gather(normed, "tp", axis=1, tiled=True),
        flat_weight,
        preferred_element_type=jnp.float32,
    )
    kv_local = (
        (summed + kv_bias.reshape(-1)[None, :])
        .astype(jnp.bfloat16)
        .reshape(tok, 2, kv_weight.shape[2])
    )
    kv_heads = kv_weight.shape[2] // HD
    group = queries.shape[1] // HD // kv_heads
    qrows = queries.reshape(tok, kv_heads, group, HD)
    device = lax.axis_index("ctx")
    ends = jnp.cumsum(lengths)
    score_scale = HD ** (-0.5)

    def docs_of(first):
        positions = first + jnp.arange(tok, dtype=jnp.int32)
        found = jnp.sum((positions[:, None] >= ends[None, :]).astype(jnp.int32), axis=1)
        return (found, positions)

    qdoc, qpos = docs_of(device * tok)

    def attend(state, block, back):
        best, mass, acc = state
        kdoc, kpos = docs_of((device - back) * tok)
        kdoc = jnp.where(device - back >= 0, kdoc, -1)
        keys = block[:, 0].reshape(tok, kv_heads, HD)
        values = block[:, 1].reshape(tok, kv_heads, HD)
        scores = (
            jnp.einsum("qgjd,kgd->gjqk", qrows, keys, preferred_element_type=jnp.float32)
            * score_scale
        )
        visible = (qdoc[:, None] == kdoc[None, :]) & (kpos[None, :] <= qpos[:, None])
        scores = jnp.where(visible[None, None], scores, -1e30)
        top = jnp.maximum(best, jnp.max(scores, axis=-1))
        probs = jnp.exp(scores - top[..., None])
        shrink = jnp.exp(best - top)
        mass = mass * shrink + jnp.sum(probs, axis=-1)
        acc = acc * shrink[..., None] + jnp.einsum(
            "gjqk,kgd->gjqd", probs.astype(jnp.bfloat16), values, preferred_element_type=jnp.float32
        )
        return (top, mass, acc)

    state = (
        jnp.full((kv_heads, group, tok), -1e30, jnp.float32),
        jnp.zeros((kv_heads, group, tok), jnp.float32),
        jnp.zeros((kv_heads, group, tok, HD), jnp.float32),
    )
    state = attend(state, kv_local, 0)
    moving = kv_local
    for back in range(1, CYCLE + 1):
        moving = shifted(moving, "ctx", 1)
        state = attend(state, moving, back)
    best, mass, acc = state
    result = acc / mass[..., None]
    return result.transpose(2, 0, 1, 3).reshape(tok, queries.shape[1]).astype(jnp.bfloat16)


def solution(mesh):
    in_specs = (P("ctx", "tp"), P("ctx", "tp"), P(), P("tp"), P(None, None, "tp"), P(None, "tp"))
    out_specs = P("ctx", "tp")
    return jax.shard_map(body, mesh=mesh, in_specs=in_specs, out_specs=out_specs, check_vma=False)
```

profile of v0, /device:TPU:4, one launch (start us, length us, event | category | flops | bytes accessed | tf_op | source)
XLA Modules:
  0.0 223.8 jit_solution(11458401559064904060)
XLA Ops:
  8.3 6.6 %psum.7 = f32[512]{0:T(512)S(1)} all-reduce(f32[512]{0:T(512)S(1)} %fusion.30), channel_id=1, replica_groups=mesh['ctx'=64,'tp'=4] {'tp'}, use_global_device_ids=true, to_apply=%region_4.5 | all-reduce | flops 512 | bytes 4096 | tf_op jit(solution)/shard_map/psum | solution.py:20
  14.9 2.7 %fusion.32 = bf16[512,1280]{1,0:T(8,128)(2,1)} fusion(bf16[512,1280]{1,0:T(8,128)(2,1)} %param.6, f32[1280]{0:T(1024)} %param.9, f32[512]{0:T(512)S(1)} %add_rsqrt_fusion), kind=kLoop, calls=%fused_computation.39 | loop fusion | flops 2621440 | bytes 2628608 | tf_op jit(solution)/shard_map/convert_element_type | solution.py:22
  18.8 5.7 %copy.82 = bf16[640,8,2,256]{3,1,2,0:T(8,128)(2,1)} copy(bf16[640,8,2,256]{3,2,1,0:T(2,128)(2,1)} %bitcast.263) | data formatting | bytes 10485760
  27.8 49.7 %all-gather.2.cloned.1.call-done = bf16[512,5120]{1,0:T(8,128)(2,1)} async-done(((bf16[512,1280]{1,0:T(8,128)(2,1)}), bf16[512,5120]{1,0:T(8,128)(2,1)}) %all-gather.2.cloned.1.call-update) | async-done | bytes 5242896 | tf_op jit(solution)/shard_map/all_gather | solution.py:25
  77.5 7.0 %fusion.41 = bf16[512,512]{0,1:T(8,128)(2,1)S(1)} fusion(bf16[512,5120]{1,0:T(8,128)(2,1)} %all-gather.2.cloned.1.call-done, bf16[5120,512]{1,0:T(8,128)(2,1)} %bitcast.264, f32[512]{0:T(512)S(1)} %bitcast.279), kind=kOutput, calls=%fused_computation.52 | convolution fusion | flops 2684878848 | bytes 11012096 | tf_op jit(solution)/shard_map/dot_general | solution.py:24
  84.5 3.5 %collective-permute-start = (bf16[512,2,256]{0,2,1:T(8,128)(2,1)S(1)}, bf16[512,2,256]{0,2,1:T(8,128)(2,1)S(1)}, u32[]{:S(2)}, u32[]{:S(2)}) collective-permute-start(bf16[512,2,256]{0,2,1:T(8,128)(2,1)S(1)} %bitcast.271), channel_id=1, source_target_pairs={{0,4},{4,8},{8,12},{12,16},{16,20},{20,24},{24,28},{28,32},{32,36}... | collective-permute-start | bytes 1572872 | tf_op jit(solution)/shard_map/ppermute | solution.py:14
  90.6 16.3 %collective-permute-done = bf16[512,2,256]{0,2,1:T(8,128)(2,1)S(1)} collective-permute-done((bf16[512,2,256]{0,2,1:T(8,128)(2,1)S(1)}, bf16[512,2,256]{0,2,1:T(8,128)(2,1)S(1)}, u32[]{:S(2)}, u32[]{:S(2)}) %collective-permute-start) | collective-permute-done | bytes 524320 | tf_op jit(solution)/shard_map/ppermute | solution.py:14
  109.6 5.7 %fusion.11 = (f32[2,5,512]{2,1,0:T(8,128)S(1)}, f32[2,512,512,5]{2,1,3,0:T(8,128)}) fusion(pred[512,512]{0,1:T(8,128)(4,1)S(1)} %get-tuple-element.35, bf16[512,2,128,1]{0,2,3,1:T(8,128)(2,1)S(1)} %bitcast.268, bf16[512,2,5,128]{0,3,2,1:T(8,128)(2,1)S(1)} %bitcast.251), kind=kOutput, calls=%fused_computation.21 | convolution fusion | flops 678947840 | bytes 12341248 | tf_op jit(solution)/shard_map/qgjd,kgd->gjqk/dot_general | solution.py:55
  115.3 13.2 %collective-permute-done.1 = bf16[512,2,256]{0,2,1:T(8,128)(2,1)S(1)} collective-permute-done((bf16[512,2,256]{0,2,1:T(8,128)(2,1)S(1)}, bf16[512,2,256]{0,2,1:T(8,128)(2,1)S(1)}, u32[]{:S(2)}, u32[]{:S(2)}) %collective-permute-start.1) | collective-permute-done | bytes 524320 | tf_op jit(solution)/shard_map/ppermute | solution.py:14
  131.3 5.9 %fusion.12 = (f32[2,5,512]{2,1,0:T(8,128)S(1)}, f32[2,512,512,5]{2,1,3,0:T(8,128)}) fusion(pred[512,512]{0,1:T(8,128)(4,1)S(1)} %get-tuple-element.32, bf16[512,2,128,1]{0,2,3,1:T(8,128)(2,1)S(1)} %bitcast.269, bf16[512,2,5,128]{0,3,2,1:T(8,128)(2,1)S(1)} %bitcast.252), kind=kOutput, calls=%fused_computation.22 | convolution fusion | flops 678947840 | bytes 12341248 | tf_op jit(solution)/shard_map/qgjd,kgd->gjqk/dot_general | solution.py:55
  137.2 12.0 %collective-permute-done.2 = bf16[512,2,256]{0,2,1:T(8,128)(2,1)S(1)} collective-permute-done((bf16[512,2,256]{0,2,1:T(8,128)(2,1)S(1)}, bf16[512,2,256]{0,2,1:T(8,128)(2,1)S(1)}, u32[]{:S(2)}, u32[]{:S(2)}) %collective-permute-start.2) | collective-permute-done | bytes 524320 | tf_op jit(solution)/shard_map/ppermute | solution.py:14
  151.8 5.9 %fusion.13 = (f32[2,5,512]{2,1,0:T(8,128)S(1)}, f32[2,512,512,5]{2,1,3,0:T(8,128)}) fusion(pred[512,512]{0,1:T(8,128)(4,1)S(1)} %get-tuple-element.33, bf16[512,2,128,1]{0,2,3,1:T(8,128)(2,1)S(1)} %bitcast.270, bf16[512,2,5,128]{0,3,2,1:T(8,128)(2,1)S(1)} %bitcast.253), kind=kOutput, calls=%fused_computation.23 | convolution fusion | flops 678947840 | bytes 12341248 | tf_op jit(solution)/shard_map/qgjd,kgd->gjqk/dot_general | solution.py:55
  157.7 11.3 %collective-permute-done.3 = bf16[512,2,256]{0,2,1:T(8,128)(2,1)S(1)} collective-permute-done((bf16[512,2,256]{0,2,1:T(8,128)(2,1)S(1)}, bf16[512,2,256]{0,2,1:T(8,128)(2,1)S(1)}, u32[]{:S(2)}, u32[]{:S(2)}) %collective-permute-start.3) | collective-permute-done | bytes 524320 | tf_op jit(solution)/shard_map/ppermute | solution.py:14
  169.7 5.7 %fusion.14 = (f32[2,5,512]{2,1,0:T(8,128)S(1)}, f32[2,512,512,5]{2,1,3,0:T(8,128)}) fusion(pred[512,512]{0,1:T(8,128)(4,1)S(1)} %get-tuple-element.34, bf16[512,2,128,1]{0,2,3,1:T(8,128)(2,1)S(1)} %bitcast.266, bf16[512,2,5,128]{0,3,2,1:T(8,128)(2,1)S(1)} %bitcast.254), kind=kOutput, calls=%fused_computation.24 | convolution fusion | flops 678947840 | bytes 12341248 | tf_op jit(solution)/shard_map/qgjd,kgd->gjqk/dot_general | solution.py:55
  176.1 2.2 fusion
  178.3 5.7 %fusion.23 = f32[2,5,512,128]{2,3,1,0:T(8,128)} fusion(bf16[512,2,128,1]{0,2,3,1:T(8,128)(2,1)} %bitcast.273, f32[2,512,512,5]{2,1,3,0:T(8,128)S(1)} %get-tuple-element.45, f32[2,5,512]{2,1,0:T(8,128)S(1)} %get-tuple-element.30, pred[512,512]{0,1:T(8,128)(4,1)S(1)} %get-tuple-element.31), kind=kOutput, calls=%fused_computation.29 | convolution fusion | flops 681574400 | bytes 13651968 | tf_op jit(solution)/shard_map/gjqk,kgd->gjqd/dot_general | solution.py:64
  184.0 3.0 %fusion.2 = f32[2,5,512]{2,1,0:T(8,128)S(1)} fusion(f32[2,512,512,5]{2,1,3,0:T(8,128)S(1)} %bitcast.256, f32[2,5,512]{2,1,0:T(8,128)} %get-tuple-element.17, pred[512,512]{0,1:T(8,128)(4,1)S(1)} %get-tuple-element.35), kind=kLoop, calls=%fused_computation.12 | loop fusion | flops 10480640 | bytes 10788864 | tf_op jit(solution)/shard_map/reduce_sum | solution.py:63
  187.1 5.0 %fusion.21 = f32[2,5,512,128]{2,3,1,0:T(8,128)} fusion(bf16[512,2,128,1]{0,2,3,1:T(8,128)(2,1)S(1)} %bitcast.275, f32[2,512,512,5]{2,1,3,0:T(8,128)S(1)} %bitcast.256, f32[2,5,512]{2,1,0:T(8,128)} %get-tuple-element.17, pred[512,512]{0,1:T(8,128)(4,1)S(1)} %get-tuple-element.35), kind=kOutput, calls=%fused_computation.28 | convolution fusion | flops 681574400 | bytes 13651968 | tf_op jit(solution)/shard_map/gjqk,kgd->gjqd/dot_general | solution.py:64
  192.1 3.6 %fusion.4 = f32[2,5,512]{2,1,0:T(8,128)} fusion(f32[2,512,512,5]{2,1,3,0:T(8,128)S(1)} %bitcast.260, f32[2,5,512]{2,1,0:T(8,128)} %get-tuple-element.16, pred[512,512]{0,1:T(8,128)(4,1)S(1)} %get-tuple-element.32), kind=kLoop, calls=%fused_computation.14 | loop fusion | flops 10480640 | bytes 10788864 | tf_op jit(solution)/shard_map/reduce_sum | solution.py:63
  195.8 5.0 %fusion.19 = f32[2,5,512,128]{2,3,1,0:T(8,128)} fusion(bf16[512,2,128,1]{0,2,3,1:T(8,128)(2,1)S(1)} %bitcast.276, f32[2,512,512,5]{2,1,3,0:T(8,128)S(1)} %bitcast.260, f32[2,5,512]{2,1,0:T(8,128)} %get-tuple-element.16, pred[512,512]{0,1:T(8,128)(4,1)S(1)} %get-tuple-element.32), kind=kOutput, calls=%fused_computation.27 | convolution fusion | flops 681574400 | bytes 13651968 | tf_op jit(solution)/shard_map/gjqk,kgd->gjqd/dot_general | solution.py:64
  200.8 2.2 fusion.6
  203.0 4.0 %fusion.17 = f32[2,5,512,128]{2,3,1,0:T(8,128)} fusion(bf16[512,2,128,1]{0,2,3,1:T(8,128)(2,1)S(1)} %bitcast.277, f32[2,512,512,5]{2,1,3,0:T(8,128)S(1)} %bitcast.262, f32[2,5,512]{2,1,0:T(8,128)S(1)} %get-tuple-element.15, pred[512,512]{0,1:T(8,128)(4,1)S(1)} %get-tuple-element.33), kind=kOutput, calls=%fused_computation.26 | convolution fusion | flops 681574400 | bytes 13651968 | tf_op jit(solution)/shard_map/gjqk,kgd->gjqd/dot_general | solution.py:64
  207.1 2.2 fusion.8
  210.4 5.1 %fusion.34 = bf16[512,2,5,128]{0,3,2,1:T(8,128)(2,1)S(1)} fusion(f32[2,5,512,128]{2,3,1,0:T(8,128)} %fusion.17, f32[2,5,512,128]{2,3,1,0:T(8,128)S(1)} %copy-done.9, f32[2,5,512,128]{2,3,1,0:T(8,128)S(1)} %copy-done.8, f32[2,5,512,128]{2,3,1,0:T(8,128)S(1)} %copy-done.7, bf16[512,2,128,1]{0,2,3,1:T(8,128)(2,1)S(1)} %bitcast.274, ...), kind=kOutput, calls=%fused_computation.42 | convolution fusion | flops 688783360 | bytes 22949888 | tf_op jit(solution)/shard_map/gjqk,kgd->gjqd/dot_general | solution.py:64
  (81 shorter events, 20.8 us)
Async XLA Ops:
  6.5 18.0 %copy-start.6 = (f32[2,256]{1,0:T(2,128)S(1)}, f32[2,256]{1,0:T(2,128)}, u32[]{:S(2)}) copy-start(f32[2,256]{1,0:T(2,128)} %param.11) | copy-start | bytes 6148
  6.5 18.0 %copy-start = (bf16[512,1280]{1,0:T(8,128)(2,1)S(1)}, bf16[512,1280]{1,0:T(8,128)(2,1)}, u32[]{:S(2)}) copy-start(bf16[512,1280]{1,0:T(8,128)(2,1)} %param.7) | copy-start | bytes 3932164
  6.5 71.0 %all-gather.2.cloned.1.call-start = ((), (), s32[]{:S(2)}) async-start(), calls=%async_computation | async-start | bytes 6553600 | tf_op jit(solution)/shard_map/all_gather | solution.py:25
  84.5 22.4 %collective-permute-start = (bf16[512,2,256]{0,2,1:T(8,128)(2,1)S(1)}, bf16[512,2,256]{0,2,1:T(8,128)(2,1)S(1)}, u32[]{:S(2)}, u32[]{:S(2)}) collective-permute-start(bf16[512,2,256]{0,2,1:T(8,128)(2,1)S(1)} %bitcast.271), channel_id=1, source_target_pairs={{0,4},{4,8},{8,12},{12,16},{16,20},{20,24},{24,28},{28,32},{32,36}... | collective-permute-start | bytes 1572872 | tf_op jit(solution)/shard_map/ppermute | solution.py:14
  106.9 21.5 %collective-permute-start.1 = (bf16[512,2,256]{0,2,1:T(8,128)(2,1)S(1)}, bf16[512,2,256]{0,2,1:T(8,128)(2,1)S(1)}, u32[]{:S(2)}, u32[]{:S(2)}) collective-permute-start(bf16[512,2,256]{0,2,1:T(8,128)(2,1)S(1)} %collective-permute-done), channel_id=1, source_target_pairs={{0,4},{4,8},{8,12},{12,16},{16,20},{20,24},{24,28},{28,32},{32,36}... | collective-permute-start | bytes 1572872 | tf_op jit(solution)/shard_map/ppermute | solution.py:14
  128.5 20.7 %collective-permute-start.2 = (bf16[512,2,256]{0,2,1:T(8,128)(2,1)S(1)}, bf16[512,2,256]{0,2,1:T(8,128)(2,1)S(1)}, u32[]{:S(2)}, u32[]{:S(2)}) collective-permute-start(bf16[512,2,256]{0,2,1:T(8,128)(2,1)S(1)} %collective-permute-done.1), channel_id=1, source_target_pairs={{0,4},{4,8},{8,12},{12,16},{16,20},{20,24},{24,28},{28,32},{32,36}... | collective-permute-start | bytes 1572872 | tf_op jit(solution)/shard_map/ppermute | solution.py:14
  149.2 19.8 %collective-permute-start.3 = (bf16[512,2,256]{0,2,1:T(8,128)(2,1)S(1)}, bf16[512,2,256]{0,2,1:T(8,128)(2,1)S(1)}, u32[]{:S(2)}, u32[]{:S(2)}) collective-permute-start(bf16[512,2,256]{0,2,1:T(8,128)(2,1)S(1)} %collective-permute-done.2), channel_id=1, source_target_pairs={{0,4},{4,8},{8,12},{12,16},{16,20},{20,24},{24,28},{28,32},{32,36}... | collective-permute-start | bytes 1572872 | tf_op jit(solution)/shard_map/ppermute | solution.py:14
  176.1 7.9 %slice-start = ((s8[10485760]{0:T(1024)(128)(4,1)}), s8[4194304]{0:T(1024)(128)(4,1)S(1)}, s32[]{:S(2)}) async-start(s8[10485760]{0:T(1024)(128)(4,1)} %bitcast.255), calls=%async_computation.1 | async-start | bytes 8388608
  176.1 7.9 %slice-start.1 = ((s8[10485760]{0:T(1024)(128)(4,1)}), s8[4194304]{0:T(1024)(128)(4,1)S(1)}, s32[]{:S(2)}) async-start(s8[10485760]{0:T(1024)(128)(4,1)} %bitcast.255), calls=%async_computation.2 | async-start | bytes 8388608
  178.3 5.7 %slice-start.2 = ((s8[10485760]{0:T(1024)(128)(4,1)}), s8[2097152]{0:T(1024)(128)(4,1)S(1)}, s32[]{:S(2)}) async-start(s8[10485760]{0:T(1024)(128)(4,1)} %bitcast.255), calls=%async_computation.3 | async-start | bytes 4194304
  184.0 8.1 %slice-start.6 = ((s8[10485760]{0:T(1024)(128)(4,1)}), s8[4194304]{0:T(1024)(128)(4,1)S(1)}, s32[]{:S(2)}) async-start(s8[10485760]{0:T(1024)(128)(4,1)} %bitcast.259), calls=%async_computation.7 | async-start | bytes 8388608
  184.0 8.1 %slice-start.7 = ((s8[10485760]{0:T(1024)(128)(4,1)}), s8[4194304]{0:T(1024)(128)(4,1)S(1)}, s32[]{:S(2)}) async-start(s8[10485760]{0:T(1024)(128)(4,1)} %bitcast.259), calls=%async_computation.8 | async-start | bytes 8388608
  187.1 5.0 %slice-start.8 = ((s8[10485760]{0:T(1024)(128)(4,1)}), s8[2097152]{0:T(1024)(128)(4,1)S(1)}, s32[]{:S(2)}) async-start(s8[10485760]{0:T(1024)(128)(4,1)} %bitcast.259), calls=%async_computation.9 | async-start | bytes 4194304
  192.1 3.7 %copy-start.3 = (bf16[512,1,256]{0,2,1:T(8,128)(2,1)S(1)}, bf16[512,1,256]{0,2,1:T(8,128)(2,1)}, u32[]{:S(2)}) copy-start(bf16[512,1,256]{0,2,1:T(8,128)(2,1)} %get-tuple-element.24) | copy-start | bytes 786436
  192.1 8.7 %slice-start.9 = ((s8[10485760]{0:T(1024)(128)(4,1)}), s8[4194304]{0:T(1024)(128)(4,1)S(1)}, s32[]{:S(2)}) async-start(s8[10485760]{0:T(1024)(128)(4,1)} %bitcast.261), calls=%async_computation.10 | async-start | bytes 8388608
  192.1 8.7 %slice-start.10 = ((s8[10485760]{0:T(1024)(128)(4,1)}), s8[4194304]{0:T(1024)(128)(4,1)S(1)}, s32[]{:S(2)}) async-start(s8[10485760]{0:T(1024)(128)(4,1)} %bitcast.261), calls=%async_computation.11 | async-start | bytes 8388608
  195.8 5.0 %slice-start.11 = ((s8[10485760]{0:T(1024)(128)(4,1)}), s8[2097152]{0:T(1024)(128)(4,1)S(1)}, s32[]{:S(2)}) async-start(s8[10485760]{0:T(1024)(128)(4,1)} %bitcast.261), calls=%async_computation.12 | async-start | bytes 4194304
  195.8 7.2 %copy-start.4 = (bf16[512,1,256]{0,2,1:T(8,128)(2,1)S(1)}, bf16[512,1,256]{0,2,1:T(8,128)(2,1)}, u32[]{:S(2)}) copy-start(bf16[512,1,256]{0,2,1:T(8,128)(2,1)} %get-tuple-element.27) | copy-start | bytes 786436
  200.8 6.3 %slice-start.3 = ((s8[10485760]{0:T(1024)(128)(4,1)}), s8[4194304]{0:T(1024)(128)(4,1)S(1)}, s32[]{:S(2)}) async-start(s8[10485760]{0:T(1024)(128)(4,1)} %bitcast.257), calls=%async_computation.4 | async-start | bytes 8388608
  200.8 6.3 %slice-start.4 = ((s8[10485760]{0:T(1024)(128)(4,1)}), s8[4194304]{0:T(1024)(128)(4,1)S(1)}, s32[]{:S(2)}) async-start(s8[10485760]{0:T(1024)(128)(4,1)} %bitcast.257), calls=%async_computation.5 | async-start | bytes 8388608
  203.0 4.1 %slice-start.5 = ((s8[10485760]{0:T(1024)(128)(4,1)}), s8[2097152]{0:T(1024)(128)(4,1)S(1)}, s32[]{:S(2)}) async-start(s8[10485760]{0:T(1024)(128)(4,1)} %bitcast.257), calls=%async_computation.6 | async-start | bytes 4194304
  203.0 6.3 %copy-start.5 = (f32[2,5,512]{2,1,0:T(8,128)S(1)}, f32[2,5,512]{2,1,0:T(8,128)}, u32[]{:S(2)}) copy-start(f32[2,5,512]{2,1,0:T(8,128)} %fusion.4) | copy-start | bytes 61444
  203.0 6.4 %copy-start.1 = (bf16[512,1,256]{0,2,1:T(8,128)(2,1)S(1)}, bf16[512,1,256]{0,2,1:T(8,128)(2,1)}, u32[]{:S(2)}) copy-start(bf16[512,1,256]{0,2,1:T(8,128)(2,1)} %get-tuple-element.18) | copy-start | bytes 786436
  207.1 3.3 %copy-start.9 = (f32[2,5,512,128]{2,3,1,0:T(8,128)S(1)}, f32[2,5,512,128]{2,3,1,0:T(8,128)}, u32[]{:S(2)}) copy-start(f32[2,5,512,128]{2,3,1,0:T(8,128)} %fusion.19) | copy-start | bytes 7864324
  (3 other events, 7.9 us)
Sparse Core Ops, SparseCore 0:
  17.8 59.6 all-gather.1
where the time goes:
time: 224 us
  waiting for transfers between devices  102 us (46%)
  matrix products  56.9 us (25%)
  other arithmetic  21.9 us (10%)
  between operations  13.8 us (6%)
  local copies, waits for them, and re-layouts  12.8 us (6%)
  starting transfers between devices  9.37 us (4%)
  blocking collectives  6.6 us (3%)
    ppermute x4, waiting for transfers between devices, shifted(): lax.ppermute(value, axis, [(source, source + steps) for source in range(l...  52.7 us
    all_gather x1, waiting for transfers between devices, body(): lax.all_gather(normed, 'tp', axis=1, tiled=True)  49.7 us
    dot_general x5, matrix products, attend(): jnp.einsum('qgjd,kgd->gjqk', qrows, keys, preferred_element_type=jnp.floa...  25.1 us
    dot_general x5, matrix products, attend(): jnp.einsum('gjqk,kgd->gjqd', probs.astype(jnp.bfloat16), values, preferre...  24.8 us
    reduce_sum x5, other arithmetic, attend(): mass = mass * shrink + jnp.sum(probs, axis=-1)  13.2 us
    ppermute x4, starting transfers between devices, shifted(): lax.ppermute(value, axis, [(source, source + steps) for source in range(l...  9.37 us
    unnamed x47, local copies, waits for them, and re-layouts  7.45 us
    dot_general x1, matrix products, body(): jnp.dot(lax.all_gather(normed, 'tp', axis=1, tiled=True), flat_weight, pr...  6.97 us
  transfers between devices with their start and end apart: 5, of which 5 were waited for; matrix products, arithmetic and copies ran while one was open for 14% of the time, Pallas kernels for 0%

commit v1 on v0

--- a/solution.py
+++ b/solution.py
@@ -22,7 +22,9 @@
     normed = (xfull * scale_rows[:, None] * norm_gain[None, :]).astype(jnp.bfloat16)
     flat_weight = kv_weight.reshape(kv_weight.shape[0], -1)
     summed = jnp.dot(
-        lax.all_gather(normed, "tp", axis=1, tiled=True),
+        jnp.concatenate(
+            lax.all_to_all(jnp.stack([normed] * lax.axis_size("tp")), "tp", 0, 0), axis=1
+        ),
         flat_weight,
         preferred_element_type=jnp.float32,
     )

time: 224 us -> 215 us (0.960)
  between operations: 13.8 us -> 0.45 us
  starting transfers between devices: 9.37 us -> 14.9 us
  local copies, waits for them, and re-layouts: 12.8 us -> 16.2 us
  waiting for transfers between devices: 102 us -> 98.8 us
    all_to_all x0 -> x1, waiting for transfers between devices: none -> 50 us  [body(): lax.all_to_all(jnp.stack([normed] * lax.axis_size('tp')), 'tp', 0, 0)]
    all_gather x1 -> x0, waiting for transfers between devices: 49.7 us -> none  [body(): lax.all_gather(normed, 'tp', axis=1, tiled=True)]
    all_to_all x0 -> x1, starting transfers between devices: none -> 5.17 us  [body(): lax.all_to_all(jnp.stack([normed] * lax.axis_size('tp')), 'tp', 0, 0)]
    ppermute x4, waiting for transfers between devices: 52.7 us -> 48.8 us  [shifted(): lax.ppermute(value, axis, [(source, source + steps) for source in range(l...]
    another operation x1 -> x2, local copies, waits for them, and re-layouts: 0.11 us -> 2.88 us  [the longest x1 2.77 us: body(): jnp.stack([normed] * lax.axis_size('tp'))]
    unnamed x47 -> x49, local copies, waits for them, and re-layouts: 7.45 us -> 7.48 us
  transfers between devices with their start and end apart: 5 -> 5, of which waited for: 5 -> 5; matrix products, arithmetic and copies ran while one was open for 14% -> 15% of each run, Pallas kernels for 0% -> 0%
where the time goes in v1:
time: 215 us; the launch traced here: 214 us
  waiting for transfers between devices  98.8 us (46%)
  matrix products  56.9 us (26%)
  other arithmetic  20.1 us (9%)
  local copies, waits for them, and re-layouts  16.2 us (8%)
  starting transfers between devices  14.9 us (7%)
  blocking collectives  6.6 us (3%)
    all_to_all x1, waiting for transfers between devices, body(): lax.all_to_all(jnp.stack([normed] * lax.axis_size('tp')), 'tp', 0, 0)  50 us
    ppermute x4, waiting for transfers between devices, shifted(): lax.ppermute(value, axis, [(source, source + steps) for source in range(l...  48.8 us
    dot_general x5, matrix products, attend(): jnp.einsum('qgjd,kgd->gjqk', qrows, keys, preferred_element_type=jnp.floa...  25.1 us
    dot_general x5, matrix products, attend(): jnp.einsum('gjqk,kgd->gjqd', probs.astype(jnp.bfloat16), values, preferre...  24.8 us
    reduce_sum x5, other arithmetic, attend(): mass = mass * shrink + jnp.sum(probs, axis=-1)  13.2 us
    ppermute x4, starting transfers between devices, shifted(): lax.ppermute(value, axis, [(source, source + steps) for source in range(l...  9.73 us
    unnamed x49, local copies, waits for them, and re-layouts  7.48 us
    dot_general x1, matrix products, body(): jnp.dot(jnp.concatenate(lax.all_to_all(jnp.stack([normed] * lax.axis_size...  6.97 us
  transfers between devices with their start and end apart: 5, of which 5 were waited for; matrix products, arithmetic and copies ran while one was open for 15% of the time, Pallas kernels for 0%

profile of v1, /device:TPU:4, one launch (start us, length us, event | category | flops | bytes accessed | tf_op | source)
XLA Modules:
  0.0 213.9 jit_solution(11692860898690413542)
XLA Ops:
  1.6 6.6 %psum.7 = f32[512]{0:T(512)S(1)} all-reduce(f32[512]{0:T(512)S(1)} %fusion.30), channel_id=1, replica_groups=mesh['ctx'=64,'tp'=4] {'tp'}, use_global_device_ids=true, to_apply=%region_4.5 | all-reduce | flops 512 | bytes 4096 | tf_op jit(solution)/shard_map/psum | solution.py:20
  10.6 2.8 %stack.2 = bf16[4,512,1280]{1,2,0:T(8,128)(2,1)} broadcast(bf16[512,1280]{0,1:T(8,128)(2,1)S(1)} %copy.36), dimensions={1,2} | broadcast | bytes 6553600 | tf_op jit(solution)/shard_map/stack | solution.py:26
  13.4 5.2 %all-to-all-start = ((bf16[4,512,1280]{1,2,0:T(8,128)(2,1)}), bf16[4,512,1280]{1,2,0:T(8,128)(2,1)}, u32[]{:S(2)}, u32[]{:S(2)}) async-start(bf16[4,512,1280]{1,2,0:T(8,128)(2,1)} %stack.2), calls=%async_computation | async-start | bytes 10485760 | tf_op jit(solution)/shard_map/all_to_all | solution.py:26
  19.0 5.7 %copy.84 = bf16[640,8,2,256]{3,1,2,0:T(8,128)(2,1)} copy(bf16[640,8,2,256]{3,2,1,0:T(2,128)(2,1)} %bitcast.266) | data formatting | bytes 10485760
  28.1 50.0 %all-to-all-done = bf16[4,512,1280]{1,2,0:T(8,128)(2,1)} async-done(((bf16[4,512,1280]{1,2,0:T(8,128)(2,1)}), bf16[4,512,1280]{1,2,0:T(8,128)(2,1)}, u32[]{:S(2)}, u32[]{:S(2)}) %all-to-all-start) | async-done | bytes 5242912 | tf_op jit(solution)/shard_map/all_to_all | solution.py:26
  78.0 7.0 %fusion.41 = bf16[512,512]{0,1:T(8,128)(2,1)S(1)} fusion(bf16[512,5120]{0,1:T(8,128)(2,1)} %bitcast.3, bf16[5120,512]{1,0:T(8,128)(2,1)} %bitcast.267, f32[512]{0:T(512)S(1)} %bitcast.282), kind=kOutput, calls=%fused_computation.52 | convolution fusion | flops 2684878848 | bytes 11012096 | tf_op jit(solution)/shard_map/dot_general | solution.py:24
  85.0 3.8 %collective-permute-start = (bf16[512,2,256]{0,2,1:T(8,128)(2,1)S(1)}, bf16[512,2,256]{0,2,1:T(8,128)(2,1)S(1)}, u32[]{:S(2)}, u32[]{:S(2)}) collective-permute-start(bf16[512,2,256]{0,2,1:T(8,128)(2,1)S(1)} %bitcast.274), channel_id=1, source_target_pairs={{0,4},{4,8},{8,12},{12,16},{16,20},{20,24},{24,28},{28,32},{32,36}... | collective-permute-start | bytes 1572872 | tf_op jit(solution)/shard_map/ppermute | solution.py:14
  91.5 15.7 %collective-permute-done = bf16[512,2,256]{0,2,1:T(8,128)(2,1)S(1)} collective-permute-done((bf16[512,2,256]{0,2,1:T(8,128)(2,1)S(1)}, bf16[512,2,256]{0,2,1:T(8,128)(2,1)S(1)}, u32[]{:S(2)}, u32[]{:S(2)}) %collective-permute-start) | collective-permute-done | bytes 524320 | tf_op jit(solution)/shard_map/ppermute | solution.py:14
  109.8 5.7 %fusion.11 = (f32[2,5,512]{2,1,0:T(8,128)S(1)}, f32[2,512,512,5]{2,1,3,0:T(8,128)}) fusion(pred[512,512]{0,1:T(8,128)(4,1)S(1)} %get-tuple-element.35, bf16[512,2,128,1]{0,2,3,1:T(8,128)(2,1)S(1)} %bitcast.271, bf16[512,2,5,128]{0,3,2,1:T(8,128)(2,1)S(1)} %bitcast.254), kind=kOutput, calls=%fused_computation.21 | convolution fusion | flops 678947840 | bytes 12341248 | tf_op jit(solution)/shard_map/qgjd,kgd->gjqk/dot_general | solution.py:57
  115.5 12.1 %collective-permute-done.1 = bf16[512,2,256]{0,2,1:T(8,128)(2,1)S(1)} collective-permute-done((bf16[512,2,256]{0,2,1:T(8,128)(2,1)S(1)}, bf16[512,2,256]{0,2,1:T(8,128)(2,1)S(1)}, u32[]{:S(2)}, u32[]{:S(2)}) %collective-permute-start.1) | collective-permute-done | bytes 524320 | tf_op jit(solution)/shard_map/ppermute | solution.py:14
  130.5 5.9 %fusion.12 = (f32[2,5,512]{2,1,0:T(8,128)S(1)}, f32[2,512,512,5]{2,1,3,0:T(8,128)}) fusion(pred[512,512]{0,1:T(8,128)(4,1)S(1)} %get-tuple-element.32, bf16[512,2,128,1]{0,2,3,1:T(8,128)(2,1)S(1)} %bitcast.272, bf16[512,2,5,128]{0,3,2,1:T(8,128)(2,1)S(1)} %bitcast.255), kind=kOutput, calls=%fused_computation.22 | convolution fusion | flops 678947840 | bytes 12341248 | tf_op jit(solution)/shard_map/qgjd,kgd->gjqk/dot_general | solution.py:57
  136.4 10.9 %collective-permute-done.2 = bf16[512,2,256]{0,2,1:T(8,128)(2,1)S(1)} collective-permute-done((bf16[512,2,256]{0,2,1:T(8,128)(2,1)S(1)}, bf16[512,2,256]{0,2,1:T(8,128)(2,1)S(1)}, u32[]{:S(2)}, u32[]{:S(2)}) %collective-permute-start.2) | collective-permute-done | bytes 524320 | tf_op jit(solution)/shard_map/ppermute | solution.py:14
  149.9 5.9 %fusion.13 = (f32[2,5,512]{2,1,0:T(8,128)S(1)}, f32[2,512,512,5]{2,1,3,0:T(8,128)}) fusion(pred[512,512]{0,1:T(8,128)(4,1)S(1)} %get-tuple-element.33, bf16[512,2,128,1]{0,2,3,1:T(8,128)(2,1)S(1)} %bitcast.273, bf16[512,2,5,128]{0,3,2,1:T(8,128)(2,1)S(1)} %bitcast.256), kind=kOutput, calls=%fused_computation.23 | convolution fusion | flops 678947840 | bytes 12341248 | tf_op jit(solution)/shard_map/qgjd,kgd->gjqk/dot_general | solution.py:57
  155.8 10.1 %collective-permute-done.3 = bf16[512,2,256]{0,2,1:T(8,128)(2,1)S(1)} collective-permute-done((bf16[512,2,256]{0,2,1:T(8,128)(2,1)S(1)}, bf16[512,2,256]{0,2,1:T(8,128)(2,1)S(1)}, u32[]{:S(2)}, u32[]{:S(2)}) %collective-permute-start.3) | collective-permute-done | bytes 524320 | tf_op jit(solution)/shard_map/ppermute | solution.py:14
  166.6 5.7 %fusion.14 = (f32[2,5,512]{2,1,0:T(8,128)S(1)}, f32[2,512,512,5]{2,1,3,0:T(8,128)}) fusion(pred[512,512]{0,1:T(8,128)(4,1)S(1)} %get-tuple-element.34, bf16[512,2,128,1]{0,2,3,1:T(8,128)(2,1)S(1)} %bitcast.269, bf16[512,2,5,128]{0,3,2,1:T(8,128)(2,1)S(1)} %bitcast.257), kind=kOutput, calls=%fused_computation.24 | convolution fusion | flops 678947840 | bytes 12341248 | tf_op jit(solution)/shard_map/qgjd,kgd->gjqk/dot_general | solution.py:57
  175.2 5.7 %fusion.23 = f32[2,5,512,128]{2,3,1,0:T(8,128)} fusion(bf16[512,2,128,1]{0,2,3,1:T(8,128)(2,1)} %bitcast.276, f32[2,512,512,5]{2,1,3,0:T(8,128)S(1)} %get-tuple-element.45, f32[2,5,512]{2,1,0:T(8,128)S(1)} %get-tuple-element.30, pred[512,512]{0,1:T(8,128)(4,1)S(1)} %get-tuple-element.31), kind=kOutput, calls=%fused_computation.29 | convolution fusion | flops 681574400 | bytes 13651968 | tf_op jit(solution)/shard_map/gjqk,kgd->gjqd/dot_general | solution.py:66
  180.9 3.0 %fusion.2 = f32[2,5,512]{2,1,0:T(8,128)S(1)} fusion(f32[2,512,512,5]{2,1,3,0:T(8,128)S(1)} %bitcast.259, f32[2,5,512]{2,1,0:T(8,128)} %get-tuple-element.17, pred[512,512]{0,1:T(8,128)(4,1)S(1)} %get-tuple-element.35), kind=kLoop, calls=%fused_computation.12 | loop fusion | flops 10480640 | bytes 10788864 | tf_op jit(solution)/shard_map/reduce_sum | solution.py:65
  184.0 5.0 %fusion.21 = f32[2,5,512,128]{2,3,1,0:T(8,128)} fusion(bf16[512,2,128,1]{0,2,3,1:T(8,128)(2,1)S(1)} %bitcast.278, f32[2,512,512,5]{2,1,3,0:T(8,128)S(1)} %bitcast.259, f32[2,5,512]{2,1,0:T(8,128)} %get-tuple-element.17, pred[512,512]{0,1:T(8,128)(4,1)S(1)} %get-tuple-element.35), kind=kOutput, calls=%fused_computation.28 | convolution fusion | flops 681574400 | bytes 13651968 | tf_op jit(solution)/shard_map/gjqk,kgd->gjqd/dot_general | solution.py:66
  189.0 3.6 %fusion.4 = f32[2,5,512]{2,1,0:T(8,128)} fusion(f32[2,512,512,5]{2,1,3,0:T(8,128)S(1)} %bitcast.263, f32[2,5,512]{2,1,0:T(8,128)} %get-tuple-element.16, pred[512,512]{0,1:T(8,128)(4,1)S(1)} %get-tuple-element.32), kind=kLoop, calls=%fused_computation.14 | loop fusion | flops 10480640 | bytes 10788864 | tf_op jit(solution)/shard_map/reduce_sum | solution.py:65
  192.7 5.0 %fusion.19 = f32[2,5,512,128]{2,3,1,0:T(8,128)} fusion(bf16[512,2,128,1]{0,2,3,1:T(8,128)(2,1)S(1)} %bitcast.279, f32[2,512,512,5]{2,1,3,0:T(8,128)S(1)} %bitcast.263, f32[2,5,512]{2,1,0:T(8,128)} %get-tuple-element.16, pred[512,512]{0,1:T(8,128)(4,1)S(1)} %get-tuple-element.32), kind=kOutput, calls=%fused_computation.27 | convolution fusion | flops 681574400 | bytes 13651968 | tf_op jit(solution)/shard_map/gjqk,kgd->gjqd/dot_general | solution.py:66
  197.7 2.2 %fusion.6 = f32[2,5,512]{2,1,0:T(8,128)S(1)} fusion(f32[2,512,512,5]{2,1,3,0:T(8,128)S(1)} %bitcast.265, f32[2,5,512]{2,1,0:T(8,128)S(1)} %get-tuple-element.15, pred[512,512]{0,1:T(8,128)(4,1)S(1)} %get-tuple-element.33), kind=kLoop, calls=%fused_computation.16 | loop fusion | flops 10480640 | bytes 10788864 | tf_op jit(solution)/shard_map/reduce_sum | solution.py:65
  199.9 4.0 %fusion.17 = f32[2,5,512,128]{2,3,1,0:T(8,128)} fusion(bf16[512,2,128,1]{0,2,3,1:T(8,128)(2,1)S(1)} %bitcast.280, f32[2,512,512,5]{2,1,3,0:T(8,128)S(1)} %bitcast.265, f32[2,5,512]{2,1,0:T(8,128)S(1)} %get-tuple-element.15, pred[512,512]{0,1:T(8,128)(4,1)S(1)} %get-tuple-element.33), kind=kOutput, calls=%fused_computation.26 | convolution fusion | flops 681574400 | bytes 13651968 | tf_op jit(solution)/shard_map/gjqk,kgd->gjqd/dot_general | solution.py:66
  204.0 2.2 %fusion.8 = f32[2,5,512]{2,1,0:T(8,128)S(1)} fusion(f32[2,512,512,5]{2,1,3,0:T(8,128)S(1)} %bitcast.261, f32[2,5,512]{2,1,0:T(8,128)S(1)} %get-tuple-element.14, pred[512,512]{0,1:T(8,128)(4,1)S(1)} %get-tuple-element.34), kind=kLoop, calls=%fused_computation.18 | loop fusion | flops 10480640 | bytes 10788864 | tf_op jit(solution)/shard_map/reduce_sum | solution.py:65
  207.3 5.1 %fusion.34 = bf16[512,2,5,128]{0,3,2,1:T(8,128)(2,1)S(1)} fusion(f32[2,5,512,128]{2,3,1,0:T(8,128)} %fusion.17, f32[2,5,512,128]{2,3,1,0:T(8,128)S(1)} %copy-done.10, f32[2,5,512,128]{2,3,1,0:T(8,128)S(1)} %copy-done.9, f32[2,5,512,128]{2,3,1,0:T(8,128)S(1)} %copy-done.8, bf16[512,2,128,1]{0,2,3,1:T(8,128)(2,1)S(1)} %bitcast.277, ...), kind=kOutput, calls=%fused_computation.42 | convolution fusion | flops 688783360 | bytes 22949888 | tf_op jit(solution)/shard_map/gjqk,kgd->gjqd/dot_general | solution.py:66
  (84 shorter events, 24.5 us)
Async XLA Ops:
  9.9 8.7 %copy-start.7 = (s32[256]{0:T(256)S(1)}, s32[256]{0:T(256)}, u32[]{:S(2)}) copy-start(s32[256]{0:T(256)} %param.8) | copy-start | bytes 3076
  13.4 11.4 %copy-start.6 = (f32[2,256]{1,0:T(2,128)S(1)}, f32[2,256]{1,0:T(2,128)}, u32[]{:S(2)}) copy-start(f32[2,256]{1,0:T(2,128)} %param.11) | copy-start | bytes 6148
  13.4 11.4 %copy-start = (bf16[512,1280]{1,0:T(8,128)(2,1)S(1)}, bf16[512,1280]{1,0:T(8,128)(2,1)}, u32[]{:S(2)}) copy-start(bf16[512,1280]{1,0:T(8,128)(2,1)} %param.7) | copy-start | bytes 3932164
  13.4 64.6 %all-to-all-start = ((bf16[4,512,1280]{1,2,0:T(8,128)(2,1)}), bf16[4,512,1280]{1,2,0:T(8,128)(2,1)}, u32[]{:S(2)}, u32[]{:S(2)}) async-start(bf16[4,512,1280]{1,2,0:T(8,128)(2,1)} %stack.2), calls=%async_computation | async-start | bytes 10485760 | tf_op jit(solution)/shard_map/all_to_all | solution.py:26
  85.0 22.2 %collective-permute-start = (bf16[512,2,256]{0,2,1:T(8,128)(2,1)S(1)}, bf16[512,2,256]{0,2,1:T(8,128)(2,1)S(1)}, u32[]{:S(2)}, u32[]{:S(2)}) collective-permute-start(bf16[512,2,256]{0,2,1:T(8,128)(2,1)S(1)} %bitcast.274), channel_id=1, source_target_pairs={{0,4},{4,8},{8,12},{12,16},{16,20},{20,24},{24,28},{28,32},{32,36}... | collective-permute-start | bytes 1572872 | tf_op jit(solution)/shard_map/ppermute | solution.py:14
  107.2 20.5 %collective-permute-start.1 = (bf16[512,2,256]{0,2,1:T(8,128)(2,1)S(1)}, bf16[512,2,256]{0,2,1:T(8,128)(2,1)S(1)}, u32[]{:S(2)}, u32[]{:S(2)}) collective-permute-start(bf16[512,2,256]{0,2,1:T(8,128)(2,1)S(1)} %collective-permute-done), channel_id=1, source_target_pairs={{0,4},{4,8},{8,12},{12,16},{16,20},{20,24},{24,28},{28,32},{32,36}... | collective-permute-start | bytes 1572872 | tf_op jit(solution)/shard_map/ppermute | solution.py:14
  127.7 19.6 %collective-permute-start.2 = (bf16[512,2,256]{0,2,1:T(8,128)(2,1)S(1)}, bf16[512,2,256]{0,2,1:T(8,128)(2,1)S(1)}, u32[]{:S(2)}, u32[]{:S(2)}) collective-permute-start(bf16[512,2,256]{0,2,1:T(8,128)(2,1)S(1)} %collective-permute-done.1), channel_id=1, source_target_pairs={{0,4},{4,8},{8,12},{12,16},{16,20},{20,24},{24,28},{28,32},{32,36}... | collective-permute-start | bytes 1572872 | tf_op jit(solution)/shard_map/ppermute | solution.py:14
  147.2 18.6 %collective-permute-start.3 = (bf16[512,2,256]{0,2,1:T(8,128)(2,1)S(1)}, bf16[512,2,256]{0,2,1:T(8,128)(2,1)S(1)}, u32[]{:S(2)}, u32[]{:S(2)}) collective-permute-start(bf16[512,2,256]{0,2,1:T(8,128)(2,1)S(1)} %collective-permute-done.2), channel_id=1, source_target_pairs={{0,4},{4,8},{8,12},{12,16},{16,20},{20,24},{24,28},{28,32},{32,36}... | collective-permute-start | bytes 1572872 | tf_op jit(solution)/shard_map/ppermute | solution.py:14
  173.0 7.9 %slice-start = ((s8[10485760]{0:T(1024)(128)(4,1)}), s8[4194304]{0:T(1024)(128)(4,1)S(1)}, s32[]{:S(2)}) async-start(s8[10485760]{0:T(1024)(128)(4,1)} %bitcast.258), calls=%async_computation.1 | async-start | bytes 8388608
  173.0 7.9 %slice-start.1 = ((s8[10485760]{0:T(1024)(128)(4,1)}), s8[4194304]{0:T(1024)(128)(4,1)S(1)}, s32[]{:S(2)}) async-start(s8[10485760]{0:T(1024)(128)(4,1)} %bitcast.258), calls=%async_computation.2 | async-start | bytes 8388608
  175.2 5.7 %slice-start.2 = ((s8[10485760]{0:T(1024)(128)(4,1)}), s8[2097152]{0:T(1024)(128)(4,1)S(1)}, s32[]{:S(2)}) async-start(s8[10485760]{0:T(1024)(128)(4,1)} %bitcast.258), calls=%async_computation.3 | async-start | bytes 4194304
  180.9 8.1 %slice-start.6 = ((s8[10485760]{0:T(1024)(128)(4,1)}), s8[4194304]{0:T(1024)(128)(4,1)S(1)}, s32[]{:S(2)}) async-start(s8[10485760]{0:T(1024)(128)(4,1)} %bitcast.262), calls=%async_computation.7 | async-start | bytes 8388608
  180.9 8.1 %slice-start.7 = ((s8[10485760]{0:T(1024)(128)(4,1)}), s8[4194304]{0:T(1024)(128)(4,1)S(1)}, s32[]{:S(2)}) async-start(s8[10485760]{0:T(1024)(128)(4,1)} %bitcast.262), calls=%async_computation.8 | async-start | bytes 8388608
  184.0 5.0 %slice-start.8 = ((s8[10485760]{0:T(1024)(128)(4,1)}), s8[2097152]{0:T(1024)(128)(4,1)S(1)}, s32[]{:S(2)}) async-start(s8[10485760]{0:T(1024)(128)(4,1)} %bitcast.262), calls=%async_computation.9 | async-start | bytes 4194304
  189.0 3.7 %copy-start.3 = (bf16[512,1,256]{0,2,1:T(8,128)(2,1)S(1)}, bf16[512,1,256]{0,2,1:T(8,128)(2,1)}, u32[]{:S(2)}) copy-start(bf16[512,1,256]{0,2,1:T(8,128)(2,1)} %get-tuple-element.24) | copy-start | bytes 786436
  189.0 8.7 %slice-start.9 = ((s8[10485760]{0:T(1024)(128)(4,1)}), s8[4194304]{0:T(1024)(128)(4,1)S(1)}, s32[]{:S(2)}) async-start(s8[10485760]{0:T(1024)(128)(4,1)} %bitcast.264), calls=%async_computation.10 | async-start | bytes 8388608
  189.0 8.7 %slice-start.10 = ((s8[10485760]{0:T(1024)(128)(4,1)}), s8[4194304]{0:T(1024)(128)(4,1)S(1)}, s32[]{:S(2)}) async-start(s8[10485760]{0:T(1024)(128)(4,1)} %bitcast.264), calls=%async_computation.11 | async-start | bytes 8388608
  192.7 5.0 %slice-start.11 = ((s8[10485760]{0:T(1024)(128)(4,1)}), s8[2097152]{0:T(1024)(128)(4,1)S(1)}, s32[]{:S(2)}) async-start(s8[10485760]{0:T(1024)(128)(4,1)} %bitcast.264), calls=%async_computation.12 | async-start | bytes 4194304
  192.7 7.2 %copy-start.4 = (bf16[512,1,256]{0,2,1:T(8,128)(2,1)S(1)}, bf16[512,1,256]{0,2,1:T(8,128)(2,1)}, u32[]{:S(2)}) copy-start(bf16[512,1,256]{0,2,1:T(8,128)(2,1)} %get-tuple-element.27) | copy-start | bytes 786436
  197.7 6.3 %slice-start.3 = ((s8[10485760]{0:T(1024)(128)(4,1)}), s8[4194304]{0:T(1024)(128)(4,1)S(1)}, s32[]{:S(2)}) async-start(s8[10485760]{0:T(1024)(128)(4,1)} %bitcast.260), calls=%async_computation.4 | async-start | bytes 8388608
  197.7 6.3 %slice-start.4 = ((s8[10485760]{0:T(1024)(128)(4,1)}), s8[4194304]{0:T(1024)(128)(4,1)S(1)}, s32[]{:S(2)}) async-start(s8[10485760]{0:T(1024)(128)(4,1)} %bitcast.260), calls=%async_computation.5 | async-start | bytes 8388608
  199.9 4.1 %slice-start.5 = ((s8[10485760]{0:T(1024)(128)(4,1)}), s8[2097152]{0:T(1024)(128)(4,1)S(1)}, s32[]{:S(2)}) async-start(s8[10485760]{0:T(1024)(128)(4,1)} %bitcast.260), calls=%async_computation.6 | async-start | bytes 4194304
  199.9 6.3 %copy-start.5 = (f32[2,5,512]{2,1,0:T(8,128)S(1)}, f32[2,5,512]{2,1,0:T(8,128)}, u32[]{:S(2)}) copy-start(f32[2,5,512]{2,1,0:T(8,128)} %fusion.4) | copy-start | bytes 61444
  199.9 6.4 %copy-start.1 = (bf16[512,1,256]{0,2,1:T(8,128)(2,1)S(1)}, bf16[512,1,256]{0,2,1:T(8,128)(2,1)}, u32[]{:S(2)}) copy-start(bf16[512,1,256]{0,2,1:T(8,128)(2,1)} %get-tuple-element.18) | copy-start | bytes 786436
  (4 other events, 11.2 us)
